TPU v7x, 512 devices: a whole 4x8x8 slice. The times are simulated.
512 devices in a mesh: dp: 128 (over y, z, core), shard: 4 (over x).
Axes of the slice: x: 4, y: 8, z: 8, core: 2. Of those that a mesh axis runs over, the one named last changes fastest.
Arguments:
- acts: bfloat16 [131072, 1792], P('dp', 'shard'), may hold values from -6 to 6
- grad_out: bfloat16 [131072, 3584], P('dp', 'shard'), may hold values from -0.016479492 to 0.016479492
- projector: bfloat16 [1792, 256], P('shard'), may hold values from -6 to 6
- moment: bfloat16 [256, 3584], P(None, 'shard'), may hold values from -4 to 4
- second: bfloat16 [256, 3584], P(None, 'shard'), may hold values from 0.29882812 to 3
Outputs:
- new_projector: bfloat16 [1792, 256], P('shard')
- new_moment: bfloat16 [256, 3584], P(None, 'shard')
- new_second: bfloat16 [256, 3584], P(None, 'shard')
- weight_update: bfloat16 [1792, 3584], P('dp', 'shard')
All inputs are finite; a program needn't handle non-finite values.
Results may differ from a plain program's by a relative error of at most 0.0055.
Values may be sent and summed in bfloat16 or wider, within the bound.
A program may use at most 64 MiB of HBM per device.

v0:
```python
import jax
import jax.numpy as jnp
from jax import lax
from jax.sharding import PartitionSpec as P

D = 1792
RANK = 256


def shards(acts, grad_out, projector, moment, second):
    inv_width = 1.0 / D**0.5
    partial_value = jnp.dot(acts, projector, preferred_element_type=jnp.float32)
    summed = lax.psum(partial_value, "shard")
    proj_acts = (summed * inv_width).astype(jnp.bfloat16)
    local_grad = jnp.einsum("tr,tf->rf", proj_acts, grad_out, preferred_element_type=jnp.float32)
    proj_grad = lax.psum(local_grad, "dp")
    proj_low = proj_grad.astype(jnp.bfloat16)
    score_terms = jnp.einsum("tf,rf->tr", grad_out, proj_low, preferred_element_type=jnp.float32)
    token_scores = lax.psum(score_terms, "shard").astype(jnp.bfloat16)
    local_sub = jnp.einsum("td,tr->dr", acts, token_scores, preferred_element_type=jnp.float32)
    subspace = lax.psum(local_sub, "dp")
    gram_local = jnp.dot(
        subspace.T, subspace, precision=lax.Precision.HIGHEST, preferred_element_type=jnp.float32
    )
    gram_matrix = lax.psum(gram_local, "shard")
    mean_square = jnp.trace(gram_matrix) / (D * RANK) + 1e-06
    cubic = jnp.dot(
        subspace, gram_matrix, precision=lax.Precision.HIGHEST, preferred_element_type=jnp.float32
    )
    new_projector = (
        (1.5 * subspace - 0.5 * cubic / (mean_square * D)) / jnp.sqrt(mean_square)
    ).astype(jnp.bfloat16)
    moment_f = 0.9 * moment.astype(jnp.float32) + 0.1 * proj_grad
    second_f = 0.95 * second.astype(jnp.float32) + 0.05 * proj_grad * proj_grad
    first_fix = 1.0 - 0.9**20
    second_fix = 1.0 - 0.95**20
    direction = (moment_f / first_fix / (jnp.sqrt(second_f / second_fix) + 1e-08)).astype(
        jnp.bfloat16
    )
    row_count = D // lax.axis_size("dp")
    replica = lax.axis_index("dp")
    all_rows = lax.all_gather(projector, "shard", axis=0, tiled=True)
    own_rows = lax.dynamic_slice_in_dim(all_rows, replica * row_count, row_count, 0)
    weight_update = (
        jnp.dot(own_rows, direction, preferred_element_type=jnp.float32) / RANK**0.5
    ).astype(jnp.bfloat16)
    return (
        new_projector,
        moment_f.astype(jnp.bfloat16),
        second_f.astype(jnp.bfloat16),
        weight_update,
    )


def solution(mesh):
    in_specs = (
        P("dp", "shard"),
        P("dp", "shard"),
        P("shard", None),
        P(None, "shard"),
        P(None, "shard"),
    )
    out_specs = (P("shard", None), P(None, "shard"), P(None, "shard"), P("dp", "shard"))
    return jax.shard_map(shards, mesh=mesh, in_specs=in_specs, out_specs=out_specs, check_vma=False)
```

profile of v0, /device:TPU:8, one launch (start us, length us, event | category | flops | bytes accessed | tf_op | source)
XLA Modules:
  0.0 563.3 jit_solution(5339090869765811914)
XLA Ops:
  7.2 0.0 copy-start
  7.2 0.0 all-reduce.6.cloned.1.call-start
  7.2 2.9 fusion.22
  10.1 0.0 all-reduce.6.cloned.1.call-update
  10.1 0.0 copy-start.3
  10.1 0.0 all-reduce.8.cloned.1.call-start
  10.2 61.5 %all-reduce.6.cloned.1.call-done = f32[1024,256]{1,0:T(8,128)} async-done(((f32[1024,256]{1,0:T(8,128)}), f32[1024,256]{1,0:T(8,128)}) %all-reduce.6.cloned.1.call-update) | async-done | bytes 1048592 | tf_op jit(solution)/shard_map/psum | solution.py:13
  71.7 0.0 copy-done
  71.7 2.9 fusion.7
  74.6 0.0 all-reduce.8.cloned.1.call-update
  74.7 0.0 all-reduce.10.cloned.1.call-start
  74.7 0.0 copy-done.3
  74.7 15.0 %all_gather.3 = bf16[1792,256]{1,0:T(8,128)(2,1)} all-gather(bf16[448,256]{1,0:T(8,128)(2,1)S(1)} %copy-done.3), channel_id=1, replica_groups=mesh['dp'=128,'shard'=4] {'shard'}, dimensions={0}, use_global_device_ids=true | all-gather | bytes 1146880 | tf_op jit(solution)/shard_map/all_gather | solution.py:42
  89.8 183.2 %all-reduce.8.cloned.1.call-done = f32[256,896]{1,0:T(8,128)} async-done(((f32[256,896]{1,0:T(8,128)}), f32[256,896]{1,0:T(8,128)}) %all-reduce.8.cloned.1.call-update) | async-done | bytes 917520 | tf_op jit(solution)/shard_map/psum | solution.py:16
  273.0 1.9 convolution_bitcast_fusion
  274.9 33.3 %all-reduce.13 = bf16[1024,256]{0,1:T(8,128)(2,1)S(1)} all-reduce(f32[1024,256]{0,1:T(8,128)S(1)} %convolution_bitcast_fusion), channel_id=1, replica_groups=mesh['dp'=128,'shard'=4] {'shard'}, use_global_device_ids=true, to_apply=%region_2.0 | all-reduce | flops 262144 | bytes 1572864 | tf_op jit(solution)/shard_map/psum | solution.py:19
  308.2 0.0 copy-start.1
  308.2 2.5 convolution_bitcast_fusion.1
  310.7 0.0 all-reduce.10.cloned.1.call-update
  310.7 0.0 all-reduce.12.cloned.1.call-start
  310.8 0.0 copy-done.1
  310.8 2.6 fusion.4
  313.4 186.1 %all-reduce.10.cloned.1.call-done = f32[448,256]{1,0:T(8,128)} async-done(((f32[448,256]{1,0:T(8,128)}), f32[448,256]{1,0:T(8,128)}) %all-reduce.10.cloned.1.call-update) | async-done | bytes 458768 | tf_op jit(solution)/shard_map/psum | solution.py:21
  499.4 2.9 fusion.23
  502.3 0.0 copy-start.2
  502.3 0.0 all-reduce.12.cloned.1.call-update
  502.3 2.4 fusion.10
  504.8 47.5 %all-reduce.12.cloned.1.call-done = f32[256,256]{1,0:T(8,128)} async-done(((f32[256,256]{1,0:T(8,128)}), f32[256,256]{1,0:T(8,128)}) %all-reduce.12.cloned.1.call-update) | async-done | bytes 262160 | tf_op jit(solution)/shard_map/psum | solution.py:25
  552.2 1.6 select_reduce_fusion
  554.5 0.0 copy-done.2
  554.5 2.2 fusion.3
Async XLA Ops:
  7.2 64.6 %copy-start = (bf16[1024,896]{1,0:T(8,128)(2,1)S(1)}, bf16[1024,896]{1,0:T(8,128)(2,1)}, u32[]{:S(2)}) copy-start(bf16[1024,896]{1,0:T(8,128)(2,1)} %param.6) | copy-start | bytes 5505028
  7.2 64.5 %all-reduce.6.cloned.1.call-start = ((), (), s32[]{:S(2)}) async-start(), calls=%async_computation | async-start | bytes 2097152 | tf_op jit(solution)/shard_map/psum | solution.py:13
  10.1 64.6 %copy-start.3 = (bf16[448,256]{1,0:T(8,128)(2,1)S(1)}, bf16[448,256]{1,0:T(8,128)(2,1)}, u32[]{:S(2)}) copy-start(bf16[448,256]{1,0:T(8,128)(2,1)} %param.7) | copy-start | bytes 688132
  10.1 262.9 %all-reduce.8.cloned.1.call-start = ((), (), s32[]{:S(2)}) async-start(), calls=%async_computation.1 | async-start | bytes 1835008 | tf_op jit(solution)/shard_map/psum | solution.py:16
  74.7 424.8 %all-reduce.10.cloned.1.call-start = ((), (), s32[]{:S(2)}) async-start(), calls=%async_computation.2 | async-start | bytes 917504 | tf_op jit(solution)/shard_map/psum | solution.py:21
  308.2 2.6 copy-start.1
  310.7 241.5 %all-reduce.12.cloned.1.call-start = ((), (), s32[]{:S(2)}) async-start(), calls=%async_computation.3 | async-start | bytes 524288 | tf_op jit(solution)/shard_map/psum | solution.py:25
  502.3 52.2 %copy-start.2 = (f32[448,256]{1,0:T(8,128)S(1)}, f32[448,256]{1,0:T(8,128)}, u32[]{:S(2)}) copy-start(f32[448,256]{1,0:T(8,128)} %all-reduce.10.cloned.1.call-done) | copy-start | bytes 1376260
Sparse Core Ops, SparseCore 0:
  10.3 61.3 all-reduce.5
  75.0 197.9 all-reduce.7
  310.9 188.5 all-reduce.9
  502.5 49.7 all-reduce.11
where the time goes:
time: 564 us; the launch traced here: 563 us
  waiting for transfers between devices  478 us (85%)
  blocking collectives  48.4 us (9%)
  matrix products  17.8 us (3%)
  between operations  14.5 us (3%)
    psum x1, waiting for transfers between devices, shards(): subspace = lax.psum(local_sub, 'dp')  186 us
    psum x1, waiting for transfers between devices, shards(): proj_grad = lax.psum(local_grad, 'dp')  183 us
    psum x1, waiting for transfers between devices, shards(): summed = lax.psum(partial_value, 'shard')  61.5 us
    psum x1, waiting for transfers between devices, shards(): gram_matrix = lax.psum(gram_local, 'shard')  47.5 us
    psum x1, blocking collectives, shards(): token_scores = lax.psum(score_terms, 'shard').astype(jnp.bfloat16)  33.3 us
    all_gather x1, blocking collectives, shards(): all_rows = lax.all_gather(projector, 'shard', axis=0, tiled=True)  15 us
  transfers between devices with their start and end apart: 4, of which 4 were waited for; matrix products, arithmetic and copies ran while one was open for 1% of the time, Pallas kernels for 0%

commit v1 on v0

--- a/solution.py
+++ b/solution.py
@@ -10,7 +10,9 @@
 def shards(acts, grad_out, projector, moment, second):
     inv_width = 1.0 / D**0.5
     partial_value = jnp.dot(acts, projector, preferred_element_type=jnp.float32)
-    summed = lax.psum(partial_value, "shard")
+    summed = partial_value
+    for hop in (1, 2):
+        summed = summed + lax.ppermute(summed, "shard", [(dev, dev ^ hop) for dev in range(4)])
     proj_acts = (summed * inv_width).astype(jnp.bfloat16)
     local_grad = jnp.einsum("tr,tf->rf", proj_acts, grad_out, preferred_element_type=jnp.float32)
     proj_grad = lax.psum(local_grad, "dp")

time: 564 us -> 558 us (0.989)
  waiting for transfers between devices: 478 us -> 466 us
  starting transfers between devices: 0.16 us -> 8.58 us
    psum x1 -> x0, waiting for transfers between devices: 61.5 us -> none  [shards(): summed = lax.psum(partial_value, 'shard')]
    ppermute x0 -> x2, waiting for transfers between devices: none -> 45.9 us  [shards(): lax.ppermute(summed, 'shard', [(dev, dev ^ hop) for dev in range(4)])]
    ppermute x0 -> x2, starting transfers between devices: none -> 8.46 us  [shards(): lax.ppermute(summed, 'shard', [(dev, dev ^ hop) for dev in range(4)])]
  transfers between devices with their start and end apart: 4 -> 5, of which waited for: 4 -> 5; matrix products, arithmetic and copies ran while one was open for 1% -> 1% of each run, Pallas kernels for 0% -> 0%
where the time goes in v1:
time: 558 us; the launch traced here: 557 us
  waiting for transfers between devices  466 us (84%)
  blocking collectives  48.7 us (9%)
  matrix products  15.5 us (3%)
  between operations  14.5 us (3%)
  starting transfers between devices  8.58 us (2%)
    psum x1, waiting for transfers between devices, shards(): proj_grad = lax.psum(local_grad, 'dp')  186 us
    psum x1, waiting for transfers between devices, shards(): subspace = lax.psum(local_sub, 'dp')  186 us
    psum x1, waiting for transfers between devices, shards(): gram_matrix = lax.psum(gram_local, 'shard')  47.5 us
    ppermute x2, waiting for transfers between devices, shards(): lax.ppermute(summed, 'shard', [(dev, dev ^ hop) for dev in range(4)])  45.9 us
    psum x1, blocking collectives, shards(): token_scores = lax.psum(score_terms, 'shard').astype(jnp.bfloat16)  33.3 us
    all_gather x1, blocking collectives, shards(): all_rows = lax.all_gather(projector, 'shard', axis=0, tiled=True)  15.4 us
  transfers between devices with their start and end apart: 5, of which 5 were waited for; matrix products, arithmetic and copies ran while one was open for 1% of the time, Pallas kernels for 0%

profile of v1, /device:TPU:8, one launch (start us, length us, event | category | flops | bytes accessed | tf_op | source)
XLA Modules:
  0.0 557.3 jit_solution(18296181119820250658)
XLA Ops:
  7.2 0.0 copy-start
  7.2 0.0 all-reduce.5.cloned.1.call-start
  7.2 1.8 fusion.22
  9.1 3.4 collective-permute-start
  12.5 23.4 %collective-permute-done = f32[1024,256]{1,0:T(8,128)S(1)} collective-permute-done((f32[1024,256]{1,0:T(8,128)S(1)}, f32[1024,256]{1,0:T(8,128)S(1)}, u32[]{:S(2)}, u32[]{:S(2)}) %collective-permute-start) | collective-permute-done | bytes 1048608 | tf_op jit(solution)/shard_map/ppermute | solution.py:15
  35.9 0.1 add.32
  36.0 0.0 copy-start.3
  36.0 5.1 collective-permute-start.1
  41.1 22.5 %collective-permute-done.1 = f32[1024,256]{1,0:T(8,128)S(1)} collective-permute-done((f32[1024,256]{1,0:T(8,128)S(1)}, f32[1024,256]{1,0:T(8,128)S(1)}, u32[]{:S(2)}, u32[]{:S(2)}) %collective-permute-start.1) | collective-permute-done | bytes 1048608 | tf_op jit(solution)/shard_map/ppermute | solution.py:15
  63.6 0.0 copy-done
  63.6 1.7 fusion.7
  65.2 0.0 all-reduce.5.cloned.1.call-update
  65.3 0.0 all-reduce.7.cloned.1.call-start
  65.3 0.0 copy-done.3
  65.3 15.4 %all_gather.3 = bf16[1792,256]{1,0:T(8,128)(2,1)} all-gather(bf16[448,256]{1,0:T(8,128)(2,1)S(1)} %copy-done.3), channel_id=1, replica_groups=mesh['dp'=128,'shard'=4] {'shard'}, dimensions={0}, use_global_device_ids=true | all-gather | bytes 1146880 | tf_op jit(solution)/shard_map/all_gather | solution.py:44
  80.7 186.4 %all-reduce.5.cloned.1.call-done = f32[256,896]{1,0:T(8,128)} async-done(((f32[256,896]{1,0:T(8,128)}), f32[256,896]{1,0:T(8,128)}) %all-reduce.5.cloned.1.call-update) | async-done | bytes 917520 | tf_op jit(solution)/shard_map/psum | solution.py:18
  267.1 1.9 convolution_bitcast_fusion
  269.0 33.3 %all-reduce.10 = bf16[1024,256]{0,1:T(8,128)(2,1)S(1)} all-reduce(f32[1024,256]{0,1:T(8,128)S(1)} %convolution_bitcast_fusion), channel_id=1, replica_groups=mesh['dp'=128,'shard'=4] {'shard'}, use_global_device_ids=true, to_apply=%region_1.0 | all-reduce | flops 262144 | bytes 1572864 | tf_op jit(solution)/shard_map/psum | solution.py:21
  302.3 0.0 copy-start.1
  302.3 2.5 convolution_bitcast_fusion.1
  304.8 0.0 all-reduce.7.cloned.1.call-update
  304.8 0.0 all-reduce.9.cloned.1.call-start
  304.9 0.0 copy-done.1
  304.9 2.6 fusion.4
  307.4 186.1 %all-reduce.7.cloned.1.call-done = f32[448,256]{1,0:T(8,128)} async-done(((f32[448,256]{1,0:T(8,128)}), f32[448,256]{1,0:T(8,128)}) %all-reduce.7.cloned.1.call-update) | async-done | bytes 458768 | tf_op jit(solution)/shard_map/psum | solution.py:23
  493.5 2.9 fusion.23
  496.4 0.0 copy-start.2
  496.4 0.0 all-reduce.9.cloned.1.call-update
  496.4 2.4 fusion.10
  498.9 47.5 %all-reduce.9.cloned.1.call-done = f32[256,256]{1,0:T(8,128)} async-done(((f32[256,256]{1,0:T(8,128)}), f32[256,256]{1,0:T(8,128)}) %all-reduce.9.cloned.1.call-update) | async-done | bytes 262160 | tf_op jit(solution)/shard_map/psum | solution.py:27
  546.3 1.6 select_reduce_fusion
  548.6 0.0 copy-done.2
  548.6 2.2 fusion.3
Async XLA Ops:
  7.2 56.4 %copy-start = (bf16[1024,896]{1,0:T(8,128)(2,1)S(1)}, bf16[1024,896]{1,0:T(8,128)(2,1)}, u32[]{:S(2)}) copy-start(bf16[1024,896]{1,0:T(8,128)(2,1)} %param.6) | copy-start | bytes 5505028
  7.2 259.9 %all-reduce.5.cloned.1.call-start = ((), (), s32[]{:S(2)}) async-start(), calls=%async_computation | async-start | bytes 1835008 | tf_op jit(solution)/shard_map/psum | solution.py:18
  9.1 26.8 %collective-permute-start = (f32[1024,256]{1,0:T(8,128)S(1)}, f32[1024,256]{1,0:T(8,128)S(1)}, u32[]{:S(2)}, u32[]{:S(2)}) collective-permute-start(f32[1024,256]{1,0:T(8,128)S(1)} %fusion.22), channel_id=1, source_target_pairs={{0,1},{1,0},{2,3},{3,2},{4,5},{5,4},{6,7},{7,6},{8,9},{9,8},{10,11... | collective-permute-start | bytes 3145736 | tf_op jit(solution)/shard_map/ppermute | solution.py:15
  36.0 29.3 %copy-start.3 = (bf16[448,256]{1,0:T(8,128)(2,1)S(1)}, bf16[448,256]{1,0:T(8,128)(2,1)}, u32[]{:S(2)}) copy-start(bf16[448,256]{1,0:T(8,128)(2,1)} %param.7) | copy-start | bytes 688132
  36.0 27.6 %collective-permute-start.1 = (f32[1024,256]{1,0:T(8,128)S(1)}, f32[1024,256]{1,0:T(8,128)S(1)}, u32[]{:S(2)}, u32[]{:S(2)}) collective-permute-start(f32[1024,256]{1,0:T(8,128)S(1)} %add.32), channel_id=1, source_target_pairs={{0,2},{1,3},{2,0},{3,1},{4,6},{5,7},{6,4},{7,5},{8,10},{9,11},{10,... | collective-permute-start | bytes 3145736 | tf_op jit(solution)/shard_map/ppermute | solution.py:15
  65.3 428.3 %all-reduce.7.cloned.1.call-start = ((), (), s32[]{:S(2)}) async-start(), calls=%async_computation.1 | async-start | bytes 917504 | tf_op jit(solution)/shard_map/psum | solution.py:23
  302.3 2.6 copy-start.1
  304.8 241.5 %all-reduce.9.cloned.1.call-start = ((), (), s32[]{:S(2)}) async-start(), calls=%async_computation.2 | async-start | bytes 524288 | tf_op jit(solution)/shard_map/psum | solution.py:27
  496.4 52.2 %copy-start.2 = (f32[448,256]{1,0:T(8,128)S(1)}, f32[448,256]{1,0:T(8,128)}, u32[]{:S(2)}) copy-start(f32[448,256]{1,0:T(8,128)} %all-reduce.7.cloned.1.call-done) | copy-start | bytes 1376260
Sparse Core Ops, SparseCore 0:
  65.4 201.6 all-reduce.4
  304.9 188.5 all-reduce.6
  496.5 49.7 all-reduce.8
